TPU v7x, 128 devices: a whole 4x4x4 slice. The times are simulated.
128 devices in a mesh: seq: 16 (over y, z), batch: 8 (over x, core).
Axes of the slice: x: 4, y: 4, z: 4, core: 2. Of those that a mesh axis runs over, the one named last changes fastest.
Arguments:
- q_nope: bfloat16 [8, 64, 128, 128], P('batch', None, 'seq'), may hold values from -6 to 6
- q_rope: bfloat16 [8, 64, 128, 64], P('batch', None, 'seq'), may hold values from -8 to 8
- absorb_k: bfloat16 [128, 128, 512], P('seq'), may hold values from -0.5 to 0.5
- absorb_v: bfloat16 [128, 512, 128], P('seq'), may hold values from -0.25 to 0.25
- cache_latent: bfloat16 [8, 16384, 512], P('batch', 'seq'), may hold values from -6 to 6
- cache_rope: bfloat16 [8, 16384, 64], P('batch', 'seq'), may hold values from -8 to 8
- draft_latent: bfloat16 [8, 64, 512], P('batch'), may hold values from -6 to 6
- draft_rope: bfloat16 [8, 64, 64], P('batch'), may hold values from -6 to 6
- residual: bfloat16 [512, 7168], P('batch', 'seq'), may hold values from -1.2 to 1.2
- out_proj: bfloat16 [16384, 7168], P('seq'), may hold values from -0.046875 to 0.046875
- norm_gain: float32 [7168], replicated, may hold values from 0.5 to 1.5
- lm_head: bfloat16 [65536, 7168], P(('seq', 'batch')), may hold values from -2.4095235 to 2.4095235
- parent: int32 [8, 64], replicated, may hold values from 0 to 62, as said below
- draft_ids: int32 [8, 64], replicated, may hold values from 0 to 65535
- cache_len: int32 [8], P('batch'), may hold values from 4096 to 16384
- accept_len: int32 [8], P('batch'), may hold values from 1 to 64
Outputs:
- hidden_out: bfloat16 [512, 7168], P('batch', 'seq')
- target_logp: float32 [8, 64], P('batch')
- accepted_score: float32 [8], P('batch')
Inputs may be any that keep to these rules, and one draw needn't show every extreme that they name: parent[b, 0] = 0, and 0 <= parent[b, i] < i for i >= 1.
All inputs are finite; a program needn't handle non-finite values.
Results may differ from a plain program's by a relative error of at most 0.0095.
Values may be sent and summed in bfloat16 or wider, within the bound.
A program may use at most 256 MiB of HBM per device.

v0:
```python
import math
import jax
import jax.numpy as jnp
from jax import lax
from jax.sharding import Mesh
from jax.sharding import PartitionSpec as P

SEQ = ("seq_0", "seq_1")
BATCH = ("batch_0", "batch_1")
SEQ_BATCH = ("seq_0", "seq_1", "batch_0", "batch_1")
masked_value = -1e30
norm_epsilon = 1e-06
highest = lax.Precision.HIGHEST


def sent_together(arrays, axis, dim, along):
    ends, at = ([], 0)
    for a in arrays[:-1]:
        at += a.shape[along]
        ends.append(at)
    both = jnp.concatenate(arrays, axis=along)
    return tuple(jnp.split(lax.all_gather(both, axis, axis=dim, tiled=True), ends, axis=along))


def copy_for_each(array, axis):
    copies = jnp.broadcast_to(array, (lax.axis_size(axis), *array.shape))
    return lax.all_to_all(copies, axis, split_axis=0, concat_axis=0, tiled=True)


def over_copies(array, axis):
    everything = copy_for_each(array, axis)
    return jnp.max(everything, axis=0)


def gathered_once(array, axis):
    leaves = jax.tree.leaves(array)
    sequence = sorted(range(len(leaves)), key=lambda k: -leaves[k].size)
    width = (1, *leaves[sequence[0]].shape)[-1]
    lines = [
        jnp.pad(leaves[k].reshape(-1), (0, -leaves[k].size % width)).reshape(-1, width)
        for k in sequence
    ]
    both, at, found = (lax.all_gather(jnp.concatenate(lines), axis), 0, {})
    for k, line in zip(sequence, lines):
        piece = both[:, at : at + len(line)].reshape(len(both), -1)
        found[k] = piece[:, : leaves[k].size].reshape(-1, *leaves[k].shape)
        at += len(line)
    numbers = iter(range(len(leaves)))
    return jax.tree.map(lambda _: found[next(numbers)], array)


def combined_by_axis(array, axes, combine):
    for axis in axes:
        pieces = gathered_once(array, axis)
        array = jax.tree.map(lambda part: part[0], pieces)
        for k in range(1, lax.axis_size(axis)):
            array = combine(array, jax.tree.map(lambda part: part[k], pieces))
    return array


def ancestry_of(parents):
    draft_count = parents.shape[1]
    indices = jnp.arange(draft_count, dtype=jnp.int32)
    parent_map = (
        (parents[:, :, None] == indices[None, None, :]) & (indices[None, :, None] > 0)
    ).astype(jnp.float32)
    ancestry = jnp.broadcast_to(jnp.eye(draft_count, dtype=jnp.float32), parent_map.shape)
    for doubling in range(draft_count.bit_length() - 1):
        ancestry = ancestry + jnp.einsum("rij,rjk->rik", ancestry, parent_map, precision=highest)
        parent_map = jnp.einsum("rij,rjk->rik", parent_map, parent_map, precision=highest)
    return ancestry > 0.5


def combine_soft(earlier, later):
    top_new = jnp.maximum(earlier[0], later[0])
    mass_new = earlier[1] * jnp.exp(earlier[0] - top_new) + later[1] * jnp.exp(later[0] - top_new)
    return (top_new, mass_new, earlier[2] + later[2])


def body(
    q_nope,
    q_rope,
    absorb_k,
    absorb_v,
    cache_latent,
    cache_rope,
    draft_latent,
    draft_rope,
    residual,
    out_proj,
    norm_gain,
    lm_head,
    parent,
    draft_ids,
    cache_len,
    accept_len,
):
    requests, draft_count, local_heads, nope_width = q_nope.shape
    cache_rows = cache_latent.shape[1]
    score_scale = 1.0 / math.sqrt(nope_width + q_rope.shape[3])
    seq_index = lax.axis_index(SEQ)
    batch_index = lax.axis_index(BATCH)
    query_latent = jnp.einsum(
        "rihn,hnc->rihc", q_nope, absorb_k, preferred_element_type=jnp.float32
    ).astype(jnp.bfloat16)
    query_all, rope_all = sent_together((query_latent, q_rope), SEQ, 2, 3)
    cache_scores = jnp.einsum(
        "rihc,rtc->rhit", query_all, cache_latent, preferred_element_type=jnp.float32
    )
    cache_scores = cache_scores + jnp.einsum(
        "rihe,rte->rhit", rope_all, cache_rope, preferred_element_type=jnp.float32
    )
    positions = seq_index * cache_rows + jnp.arange(cache_rows, dtype=jnp.int32)
    in_cache = positions[None, :] < cache_len[:, None]
    cache_scores = jnp.where(in_cache[:, None, None, :], cache_scores * score_scale, masked_value)
    tree_scores = jnp.einsum(
        "rihc,rjc->rhij", query_all, draft_latent, preferred_element_type=jnp.float32
    )
    tree_scores = tree_scores + jnp.einsum(
        "rihe,rje->rhij", rope_all, draft_rope, preferred_element_type=jnp.float32
    )
    own_parents = lax.dynamic_slice_in_dim(parent, batch_index * requests, requests, 0)
    ancestry = ancestry_of(own_parents)
    tree_scores = jnp.where(ancestry[:, None, :, :], tree_scores * score_scale, masked_value)
    local_top = jnp.maximum(jnp.max(cache_scores, axis=3), jnp.max(tree_scores, axis=3))
    row_top = over_copies(local_top, SEQ)
    cache_weights = jnp.exp(cache_scores - row_top[..., None])
    weight_sum = jnp.sum(cache_weights, axis=3)
    partial_value = jnp.einsum(
        "rhit,rtc->rhic",
        cache_weights.astype(jnp.bfloat16),
        cache_latent,
        preferred_element_type=jnp.float32,
    )
    head_first = seq_index * local_heads
    tree_mine = lax.dynamic_slice_in_dim(tree_scores, head_first, local_heads, 1)
    top_mine = lax.dynamic_slice_in_dim(row_top, head_first, local_heads, 1)
    tree_weights = jnp.exp(tree_mine - top_mine[..., None])
    tree_out = jnp.einsum(
        "rhij,rjc->rhic",
        tree_weights.astype(jnp.bfloat16),
        draft_latent,
        preferred_element_type=jnp.float32,
    )
    latent_sum, weight_total = (
        lax.psum_scatter(partial_value, SEQ, scatter_dimension=1, tiled=True),
        lax.psum_scatter(weight_sum, SEQ, scatter_dimension=1, tiled=True),
    )
    summed = jnp.einsum(
        "rhic,hcn->rhin", latent_sum + tree_out, absorb_v, preferred_element_type=jnp.float32
    )
    weight_total = weight_total + jnp.sum(tree_weights, axis=3)
    head_out = (summed / weight_total[..., None]).astype(jnp.bfloat16)
    head_rows = jnp.transpose(head_out, (0, 2, 1, 3)).reshape(
        requests * draft_count, local_heads * head_out.shape[3]
    )
    branch_term = jnp.dot(head_rows, out_proj, preferred_element_type=jnp.float32)
    width_local = residual.shape[1]
    feature_first = seq_index * width_local
    residual_wide = lax.dynamic_update_slice_in_dim(
        jnp.zeros_like(branch_term), residual.astype(jnp.float32), feature_first, 1
    )
    stream = lax.psum(branch_term + residual_wide, SEQ)
    square = jnp.sum(stream * stream, axis=1)
    normed = (
        stream * lax.rsqrt(square / stream.shape[1] + norm_epsilon)[:, None] * norm_gain
    ).astype(jnp.bfloat16)
    hidden_out = lax.dynamic_slice_in_dim(stream, feature_first, width_local, 1).astype(
        jnp.bfloat16
    )
    vocab_rows = lm_head.shape[0]
    vocab_first = lax.axis_index(SEQ_BATCH) * vocab_rows
    logits = jnp.einsum(
        "rd,vd->rv",
        lax.all_gather(normed, BATCH, axis=0, tiled=True),
        lm_head,
        preferred_element_type=jnp.float32,
    )
    request_total = parent.shape[0]
    parent_rows = (
        jnp.arange(request_total, dtype=jnp.int32)[:, None] * draft_count + parent
    ).reshape(-1)
    source = logits[parent_rows]
    column = jnp.arange(vocab_rows, dtype=jnp.int32) + vocab_first
    picked = jnp.sum(
        jnp.where(column[None, :] == draft_ids.reshape(-1)[:, None], source, 0.0), axis=1
    )
    local_best = jnp.max(logits, axis=1)
    local_mass = jnp.sum(jnp.exp(logits - local_best[:, None]), axis=1)
    best, exp_mass, chosen = combined_by_axis(
        (local_best, local_mass, picked), SEQ_BATCH, combine_soft
    )
    log_total = best + jnp.log(exp_mass)
    target_all = (chosen - log_total[parent_rows]).reshape(request_total, draft_count)
    target_logp = lax.dynamic_slice_in_dim(target_all, batch_index * requests, requests, 0)
    accepted_score = jnp.sum(
        jnp.where(
            jnp.arange(draft_count, dtype=jnp.int32)[None, :] < accept_len[:, None],
            target_logp,
            0.0,
        ),
        axis=1,
    )
    return (hidden_out, target_logp, accepted_score)


def solution(mesh):
    split = Mesh(mesh.devices.reshape(4, 4, 4, 2), ("seq_0", "seq_1", "batch_0", "batch_1"))
    in_specs = (
        P(BATCH, None, SEQ, None),
        P(BATCH, None, SEQ, None),
        P(SEQ, None, None),
        P(SEQ, None, None),
        P(BATCH, SEQ, None),
        P(BATCH, SEQ, None),
        P(BATCH, None, None),
        P(BATCH, None, None),
        P(BATCH, SEQ),
        P(SEQ, None),
        P(),
        P(SEQ_BATCH, None),
        P(),
        P(),
        P(BATCH),
        P(BATCH),
    )
    out_specs = (P(BATCH, SEQ), P(BATCH, None), P(BATCH))
    return jax.shard_map(body, mesh=split, in_specs=in_specs, out_specs=out_specs, check_vma=False)
```

profile of v0, /device:TPU:1, one launch (start us, length us, event | category | flops | bytes accessed | tf_op | source)
XLA Modules:
  0.0 529.6 jit_solution(17929896783594325636)
XLA Ops:
  7.2 1.0 copy.41
  8.2 1.6 fusion.16
  9.9 0.9 maximum_bitcast_fusion
  11.5 0.7 fusion.88
  12.2 0.2 fusion.39
  12.5 0.2 convolution_add_fusion.5
  12.7 0.2 fusion.99
  12.8 0.2 convolution_add_fusion.4
  13.2 0.2 convolution_add_fusion.3
  13.9 0.2 convolution_add_fusion.1
  14.0 0.2 fusion.17
  14.3 80.4 %all-gather.11.cloned.1.call-done = bf16[1,64,128,576]{3,1,0,2:T(8,128)(2,1)} async-done(((bf16[1,64,8,576]{3,1,0,2:T(8,128)(2,1)}), bf16[1,64,128,576]{3,1,0,2:T(8,128)(2,1)}) %all-gather.11.cloned.1.call-update) | async-done | bytes 9437200 | tf_op jit(solution)/shard_map/all_gather | solution.py:22
  94.7 1.8 split.9
  96.5 2.9 copy.69
  99.4 7.5 %fusion.10 = f32[64,128,64]{0,2,1:T(8,128)S(1)} fusion(bf16[1,64,512]{2,1,0:T(8,128)(2,1)S(1)} %copy-done.5, bf16[1,64,128,576]{3,1,0,2:T(8,128)(2,1)} %all-gather.11.cloned.1.call-done), kind=kOutput, calls=%fused_computation.11 | convolution fusion | flops 536870912 | bytes 10551296 | tf_op jit(solution)/shard_map/rihc,rjc->rhij/dot_general | solution.py:116
  106.9 5.8 %fusion.97 = (f32[128,64]{1,0:T(8,128)S(1)}, f32[1,128,64,64]{2,3,1,0:T(8,128)}) fusion(f32[64,128,64]{0,2,1:T(8,128)S(1)} %fusion.10, bf16[1,64,64]{2,1,0:T(8,128)(2,1)S(1)} %copy-done.8, bf16[1,64,128,576]{3,1,0,2:T(8,128)(2,1)} %all-gather.11.cloned.1.call-done, pred[64,64]{0,1:T(8,128)(4,1)S(1)} %copy.45), kind=kOutput, calls=%fused_computation.169 | convolution fusion | flops 69197824 | bytes 6336512 | tf_op jit(solution)/shard_map/rihe,rje->rhij/dot_general | solution.py:119
  112.8 7.7 %split.8 = bf16[1,64,128,512]{3,1,0,2:T(8,128)(2,1)} slice(bf16[1,64,128,576]{3,1,0,2:T(8,128)(2,1)} %all-gather.11.cloned.1.call-done), slice={[0:1], [0:64], [0:128], [0:512]} | slice | bytes 16777216 | tf_op jit(solution)/shard_map/split | solution.py:22
  120.5 30.0 %fusion.12 = f32[64,128,1024]{2,1,0:T(8,128)} fusion(bf16[1,64,128,512]{3,1,0,2:T(8,128)(2,1)} %split.8, bf16[1,1024,512]{2,1,0:T(8,128)(2,1)S(1)} %copy-done), kind=kOutput, calls=%fused_computation.14 | convolution fusion | flops 8589934592 | bytes 42991616 | tf_op jit(solution)/shard_map/rihc,rtc->rhit/dot_general | solution.py:107
  150.5 21.9 %fusion.96 = (f32[128,64]{0,1:T(8,128)S(1)}, f32[1,128,64,1024]{3,1,2,0:T(8,128)}) fusion(f32[64,128,1024]{2,1,0:T(8,128)} %fusion.12, bf16[1,1024,64]{1,2,0:T(8,128)(2,1)S(1)} %copy-done.4, bf16[1,64,128,64]{2,3,1,0:T(8,128)(2,1)S(1)} %copy-done.3, pred[1024]{0:T(1024)(128)(4,1)S(1)} %add_compare_fusion), kind=kOutput, calls=%fused_computation.168 | convolution fusion | flops 1107288064 | bytes 68322304 | tf_op jit(solution)/shard_map/rihe,rte->rhit/dot_general | solution.py:110
  172.5 15.1 %all_to_all.5 = f32[16,1,128,64]{2,3,1,0:T(8,128)S(1)} all-to-all(f32[16,1,128,64]{2,3,1,0:T(8,128)S(1)} %broadcast_in_dim.37), channel_id=1, replica_groups=mesh['seq_0'=4,'seq_1'=4,'batch_0'=4,'batch_1'=2] {'seq_0','seq_1'}, dimensions={0} | all-to-all | bytes 1048576 | tf_op jit(solution)/shard_map/all_to_all | solution.py:27
  187.7 18.7 %fusion.7 = f32[1,128,64,512]{3,1,2,0:T(8,128)} fusion(f32[1,128,64,1024]{3,1,2,0:T(8,128)} %get-tuple-element.19, f32[128,64]{0,1:T(8,128)S(1)} %reduce_max.38, bf16[1,1024,512]{2,1,0:T(8,128)(2,1)S(1)} %copy-done), kind=kOutput, calls=%fused_computation.10 | convolution fusion | flops 8606711808 | bytes 51412992 | tf_op jit(solution)/shard_map/rhit,rtc->rhic/dot_general | solution.py:129
  206.5 0.6 copy-done.12
  207.0 0.6 dynamic-slice.5
  208.4 1.0 fusion.24
  209.5 14.9 %fusion.1 = f32[128,64]{0,1:T(8,128)S(1)} fusion(f32[1,128,64,1024]{3,1,2,0:T(8,128)} %get-tuple-element.19, f32[128,64]{0,1:T(8,128)S(1)} %reduce_max.38), kind=kLoop, calls=%fused_computation.5 | loop fusion | flops 16769024 | bytes 33619968 | tf_op jit(solution)/shard_map/reduce_sum | solution.py:128
  224.6 58.5 %all-reduce = f32[1,128,64]{2,1,0:T(8,128)S(1)} all-reduce(f32[1,128,64]{2,1,0:T(8,128)S(1)} %copy.53), channel_id=7, replica_groups=mesh['seq_0'=4,'seq_1'=4,'batch_0'=4,'batch_1'=2] {'seq_0','seq_1'}, use_global_device_ids=true, to_apply=%region_5.6.clone | all-reduce | flops 8192 | bytes 65536
  283.4 33.9 %reduce-scatter.3.cloned.1.call-done = f32[1,8,64,512]{3,1,2,0:T(8,128)} async-done(((f32[1,128,64,512]{3,1,2,0:T(8,128)}), f32[1,8,64,512]{3,1,2,0:T(8,128)}) %reduce-scatter.3.cloned.1.call-update) | async-done | bytes 1048592 | tf_op jit(solution)/shard_map/reduce_scatter | solution.py:146
  317.3 1.5 fusion.15
  318.9 0.4 fusion.19
  319.4 7.9 %fusion.27 = f32[64,7168]{1,0:T(8,128)S(1)} fusion(bf16[1024,7168]{1,0:T(8,128)(2,1)} %param.25, bf16[8,8,8,128]{3,2,1,0:T(8,128)(2,1)S(1)} %bitcast.377), kind=kOutput, calls=%fused_computation.45 | convolution fusion | flops 939524096 | bytes 16646144 | tf_op jit(solution)/shard_map/dot_general | solution.py:157
  327.4 1.1 add.352
  328.5 1.2 copy-done.2
  329.8 88.2 %all-reduce.3.cloned.1.call-done = f32[64,7168]{1,0:T(8,128)} async-done(((f32[64,7168]{1,0:T(8,128)}), f32[64,7168]{1,0:T(8,128)}) %all-reduce.3.cloned.1.call-update) | async-done | bytes 1835024 | tf_op jit(solution)/shard_map/psum | solution.py:163
  418.0 1.7 multiply_reduce_fusion
  419.7 2.7 multiply_convert_fusion
  423.3 1.6 dynamic-slice_convert_fusion
  425.0 43.8 %all-gather.13.cloned.1.call-done = bf16[512,7168]{1,0:T(8,128)(2,1)} async-done(((bf16[64,7168]{1,0:T(8,128)(2,1)}), bf16[512,7168]{1,0:T(8,128)(2,1)}) %all-gather.13.cloned.1.call-update) | async-done | bytes 7340048 | tf_op jit(solution)/shard_map/all_gather | solution.py:175
  468.8 8.5 %fusion.98 = (f32[512]{0:T(512)S(1)}, f32[512,512]{0,1:T(8,128)S(1)}) fusion(bf16[512,7168]{1,0:T(8,128)(2,1)} %all-gather.13.cloned.1.call-done, bf16[512,7168]{1,0:T(8,128)(2,1)} %param.27), kind=kOutput, calls=%fused_computation.170 | convolution fusion | flops 3758358016 | bytes 15730688 | tf_op jit(solution)/shard_map/rd,vd->rv/dot_general | solution.py:173
  477.3 0.3 copy.58
  477.6 0.2 exponential_reduce_fusion
  477.8 1.6 gather_fusion
  479.5 0.3 select_reduce_fusion
  479.7 9.6 %all-gather.4 = f32[4,3,512]{2,1,0:T(4,128)S(1)} all-gather(f32[1,3,512]{2,1,0:T(4,128)S(1)} %maximum_bitcast_fusion.1), channel_id=2, replica_groups=mesh['seq_0'=4,'seq_1'=4,'batch_0'=4,'batch_1'=2] {'seq_0'}, dimensions={0}, use_global_device_ids=true | all-gather | bytes 30720 | tf_op jit(solution)/shard_map/all_gather | solution.py:43
  489.4 9.5 %all-gather.5 = f32[4,3,512]{2,1,0:T(4,128)S(1)} all-gather(f32[1,3,512]{2,1,0:T(4,128)S(1)} %maximum_bitcast_fusion.2), channel_id=3, replica_groups=mesh['seq_0'=4,'seq_1'=4,'batch_0'=4,'batch_1'=2] {'seq_1'}, dimensions={0}, use_global_device_ids=true | all-gather | bytes 30720 | tf_op jit(solution)/shard_map/all_gather | solution.py:43
  498.9 9.0 %all-gather.6 = f32[4,3,512]{2,1,0:T(4,128)S(1)} all-gather(f32[1,3,512]{2,1,0:T(4,128)S(1)} %maximum_bitcast_fusion.3), channel_id=4, replica_groups=mesh['seq_0'=4,'seq_1'=4,'batch_0'=4,'batch_1'=2] {'batch_0'}, dimensions={0}, use_global_device_ids=true | all-gather | bytes 30720 | tf_op jit(solution)/shard_map/all_gather | solution.py:43
  508.0 10.2 %all-gather.7 = f32[2,3,512]{2,1,0:T(4,128)S(1)} all-gather(f32[1,3,512]{2,1,0:T(4,128)S(1)} %maximum_bitcast_fusion.4), channel_id=5, replica_groups=mesh['seq_0'=4,'seq_1'=4,'batch_0'=4,'batch_1'=2] {'batch_1'}, dimensions={0}, use_global_device_ids=true | all-gather | bytes 18432 | tf_op jit(solution)/shard_map/all_gather | solution.py:43
  518.3 3.5 gather_fusion.1
  521.9 1.1 fusion.89
  (77 shorter events, 2.6 us)
Async XLA Ops:
  7.2 113.3 %copy-start = (bf16[1,1024,512]{2,1,0:T(8,128)(2,1)S(1)}, bf16[1,1024,512]{2,1,0:T(8,128)(2,1)}, u32[]{:S(2)}) copy-start(bf16[1,1024,512]{2,1,0:T(8,128)(2,1)} %param.20) | copy-start | bytes 3145732
  7.2 92.3 %copy-start.5 = (bf16[1,64,512]{2,1,0:T(8,128)(2,1)S(1)}, bf16[1,64,512]{2,1,0:T(8,128)(2,1)}, u32[]{:S(2)}) copy-start(bf16[1,64,512]{2,1,0:T(8,128)(2,1)} %param.22) | copy-start | bytes 196612
  7.2 87.5 %all-gather.11.cloned.1.call-start = ((), (), s32[]{:S(2)}) async-start(), calls=%async_computation.2 | async-start | bytes 11141120 | tf_op jit(solution)/shard_map/all_gather | solution.py:22
  10.8 306.5 %reduce-scatter.3.cloned.1.call-start = ((), (), s32[]{:S(2)}) async-start(), calls=%async_computation.3 | async-start | bytes 17825792 | tf_op jit(solution)/shard_map/reduce_scatter | solution.py:146
  96.5 10.4 %copy-start.8 = (bf16[1,64,64]{2,1,0:T(8,128)(2,1)S(1)}, bf16[1,64,64]{2,1,0:T(8,128)(2,1)}, u32[]{:S(2)}) copy-start(bf16[1,64,64]{2,1,0:T(8,128)(2,1)} %param.23) | copy-start | bytes 24580
  120.5 30.0 %copy-start.3 = (bf16[1,64,128,64]{2,3,1,0:T(8,128)(2,1)S(1)}, bf16[1,64,128,64]{2,3,1,0:T(8,128)(2,1)}, u32[]{:S(2)}) copy-start(bf16[1,64,128,64]{2,3,1,0:T(8,128)(2,1)} %copy.69) | copy-start | bytes 3145732
  120.5 30.0 %copy-start.4 = (bf16[1,1024,64]{1,2,0:T(8,128)(2,1)S(1)}, bf16[1,1024,64]{1,2,0:T(8,128)(2,1)}, u32[]{:S(2)}) copy-start(bf16[1,1024,64]{1,2,0:T(8,128)(2,1)} %param.21) | copy-start | bytes 393220
  206.4 0.7 copy-start.12
  206.4 211.5 %all-reduce.3.cloned.1.call-start = ((), (), s32[]{:S(2)}) async-start(), calls=%async_computation.4 | async-start | bytes 3670016 | tf_op jit(solution)/shard_map/psum | solution.py:163
  209.5 109.3 %copy-start.11 = (bf16[8,512,128]{2,1,0:T(8,128)(2,1)S(1)}, bf16[8,512,128]{2,1,0:T(8,128)(2,1)}, u32[]{:S(2)}) copy-start(bf16[8,512,128]{2,1,0:T(8,128)(2,1)} %param.19) | copy-start | bytes 3145732
  319.3 7.9 %copy-start.6 = (bf16[64,448]{1,0:T(8,128)(2,1)S(1)}, bf16[64,448]{1,0:T(8,128)(2,1)}, u32[]{:S(2)}) copy-start(bf16[64,448]{1,0:T(8,128)(2,1)} %param.24) | copy-start | bytes 172036
  319.3 100.3 %copy-start.7 = (f32[7168]{0:T(1024)S(1)}, f32[7168]{0:T(1024)}, u32[]{:S(2)}) copy-start(f32[7168]{0:T(1024)} %param.26) | copy-start | bytes 86020
  319.4 103.7 %copy-start.9 = (s32[8,64]{1,0:T(8,128)S(1)}, s32[8,64]{1,0:T(8,128)}, u32[]{:S(2)}) copy-start(s32[8,64]{1,0:T(8,128)} %param.29) | copy-start | bytes 6148
  319.4 103.8 %copy-start.10 = (s32[8,64]{1,0:T(8,128)S(1)}, s32[8,64]{1,0:T(8,128)}, u32[]{:S(2)}) copy-start(s32[8,64]{1,0:T(8,128)} %param.28) | copy-start | bytes 6148
  328.5 1.3 copy-start.2
  329.7 139.0 %all-gather.13.cloned.1.call-start = ((), (), s32[]{:S(2)}) async-start(), calls=%async_computation.5 | async-start | bytes 8257536 | tf_op jit(solution)/shard_map/all_gather | solution.py:175
  468.8 54.3 %copy-start.1 = (bf16[1,1024,512]{2,1,0:T(8,128)(2,1)S(1)}, bf16[1,1024,512]{2,1,0:T(8,128)(2,1)}, u32[]{:S(2)}) copy-start(bf16[1,1024,512]{2,1,0:T(8,128)(2,1)} %param.20) | copy-start | bytes 3145732
Sparse Core Ops, SparseCore 0:
  10.9 83.7 all-gather.10
  206.5 110.7 reduce-scatter.2
  329.9 88.0 all-reduce.2
  422.5 46.2 all-gather.12
where the time goes:
time: 530 us
  waiting for transfers between devices  246 us (46%)
  blocking collectives  112 us (21%)
  matrix products  106 us (20%)
  local copies, waits for them, and re-layouts  26 us (5%)
  other arithmetic  23.3 us (4%)
  between operations  16.1 us (3%)
    psum x1, waiting for transfers between devices, body(): stream = lax.psum(branch_term + residual_wide, SEQ)  88.2 us
    all_gather x1, waiting for transfers between devices, sent_together(): lax.all_gather(both, axis, axis=dim, tiled=True)  80.4 us
    unnamed x1, blocking collectives  58.5 us
    all_gather x1, waiting for transfers between devices, body(): lax.all_gather(normed, BATCH, axis=0, tiled=True)  43.8 us
    all_gather x4, blocking collectives, gathered_once(): both, at, found = (lax.all_gather(jnp.concatenate(lines), axis), 0, {})  38.3 us
    reduce_scatter x1, waiting for transfers between devices, body(): lax.psum_scatter(partial_value, SEQ, scatter_dimension=1, tiled=True)  33.9 us
    dot_general x1, matrix products, body(): jnp.einsum('rihc,rtc->rhit', query_all, cache_latent, preferred_element_t...  30 us
    dot_general x1, matrix products, body(): jnp.einsum('rihe,rte->rhit', rope_all, cache_rope, preferred_element_type...  21.9 us
  transfers between devices with their start and end apart: 4, of which 4 were waited for; matrix products, arithmetic and copies ran while one was open for 4% of the time, Pallas kernels for 0%

commit v1 on v0

--- a/solution.py
+++ b/solution.py
@@ -160,7 +160,7 @@
     residual_wide = lax.dynamic_update_slice_in_dim(
         jnp.zeros_like(branch_term), residual.astype(jnp.float32), feature_first, 1
     )
-    stream = lax.psum(branch_term + residual_wide, SEQ)
+    stream = lax.psum(lax.psum(branch_term + residual_wide, "seq_0"), "seq_1")
     square = jnp.sum(stream * stream, axis=1)
     normed = (
         stream * lax.rsqrt(square / stream.shape[1] + norm_epsilon)[:, None] * norm_gain

time: 530 us -> 552 us (1.042)
  waiting for transfers between devices: 246 us -> 268 us
    psum x1 -> x2, waiting for transfers between devices: 88.2 us -> 111 us  [body(): stream = lax.psum(lax.psum(branch_term + residual_wide, 'seq_0'), 'seq_1')]
  transfers between devices with their start and end apart: 4 -> 5, of which waited for: 4 -> 5; matrix products, arithmetic and copies ran while one was open for 4% -> 4% of each run, Pallas kernels for 0% -> 0%
where the time goes in v1:
time: 552 us
  waiting for transfers between devices  268 us (49%)
  blocking collectives  112 us (20%)
  matrix products  106 us (19%)
  local copies, waits for them, and re-layouts  25.9 us (5%)
  other arithmetic  23.3 us (4%)
  between operations  16.2 us (3%)
    psum x2, waiting for transfers between devices, body(): stream = lax.psum(lax.psum(branch_term + residual_wide, 'seq_0'), 'seq_1')  111 us
    all_gather x1, waiting for transfers between devices, sent_together(): lax.all_gather(both, axis, axis=dim, tiled=True)  80.4 us
    unnamed x1, blocking collectives  58.5 us
    all_gather x1, waiting for transfers between devices, body(): lax.all_gather(normed, BATCH, axis=0, tiled=True)  43 us
    all_gather x4, blocking collectives, gathered_once(): both, at, found = (lax.all_gather(jnp.concatenate(lines), axis), 0, {})  38.3 us
    reduce_scatter x1, waiting for transfers between devices, body(): lax.psum_scatter(partial_value, SEQ, scatter_dimension=1, tiled=True)  33.9 us
    dot_general x1, matrix products, body(): jnp.einsum('rihc,rtc->rhit', query_all, cache_latent, preferred_element_t...  30 us
    dot_general x1, matrix products, body(): jnp.einsum('rihe,rte->rhit', rope_all, cache_rope, preferred_element_type...  21.9 us
  transfers between devices with their start and end apart: 5, of which 5 were waited for; matrix products, arithmetic and copies ran while one was open for 4% of the time, Pallas kernels for 0%

profile of v1, /device:TPU:1, one launch (start us, length us, event | category | flops | bytes accessed | tf_op | source)
XLA Modules:
  0.0 551.6 jit_solution(4770908249126107364)
XLA Ops:
  7.2 1.0 copy.41
  8.2 1.6 fusion.16
  9.9 0.9 maximum_bitcast_fusion
  11.5 0.7 fusion.88
  12.2 0.2 fusion.39
  12.5 0.2 convolution_add_fusion.5
  12.7 0.2 fusion.99
  12.8 0.2 convolution_add_fusion.4
  13.9 0.2 convolution_add_fusion.1
  14.0 0.2 fusion.17
  14.3 80.4 %all-gather.11.cloned.1.call-done = bf16[1,64,128,576]{3,1,0,2:T(8,128)(2,1)} async-done(((bf16[1,64,8,576]{3,1,0,2:T(8,128)(2,1)}), bf16[1,64,128,576]{3,1,0,2:T(8,128)(2,1)}) %all-gather.11.cloned.1.call-update) | async-done | bytes 9437200 | tf_op jit(solution)/shard_map/all_gather | solution.py:22
  94.7 1.8 split.9
  96.5 2.9 copy.69
  99.4 7.5 %fusion.10 = f32[64,128,64]{0,2,1:T(8,128)S(1)} fusion(bf16[1,64,512]{2,1,0:T(8,128)(2,1)S(1)} %copy-done.5, bf16[1,64,128,576]{3,1,0,2:T(8,128)(2,1)} %all-gather.11.cloned.1.call-done), kind=kOutput, calls=%fused_computation.11 | convolution fusion | flops 536870912 | bytes 10551296 | tf_op jit(solution)/shard_map/rihc,rjc->rhij/dot_general | solution.py:116
  106.9 5.8 %fusion.97 = (f32[128,64]{1,0:T(8,128)S(1)}, f32[1,128,64,64]{2,3,1,0:T(8,128)}) fusion(f32[64,128,64]{0,2,1:T(8,128)S(1)} %fusion.10, bf16[1,64,64]{2,1,0:T(8,128)(2,1)S(1)} %copy-done.8, bf16[1,64,128,576]{3,1,0,2:T(8,128)(2,1)} %all-gather.11.cloned.1.call-done, pred[64,64]{0,1:T(8,128)(4,1)S(1)} %copy.45), kind=kOutput, calls=%fused_computation.169 | convolution fusion | flops 69197824 | bytes 6336512 | tf_op jit(solution)/shard_map/rihe,rje->rhij/dot_general | solution.py:119
  112.8 7.7 %split.8 = bf16[1,64,128,512]{3,1,0,2:T(8,128)(2,1)} slice(bf16[1,64,128,576]{3,1,0,2:T(8,128)(2,1)} %all-gather.11.cloned.1.call-done), slice={[0:1], [0:64], [0:128], [0:512]} | slice | bytes 16777216 | tf_op jit(solution)/shard_map/split | solution.py:22
  120.5 30.0 %fusion.12 = f32[64,128,1024]{2,1,0:T(8,128)} fusion(bf16[1,64,128,512]{3,1,0,2:T(8,128)(2,1)} %split.8, bf16[1,1024,512]{2,1,0:T(8,128)(2,1)S(1)} %copy-done), kind=kOutput, calls=%fused_computation.14 | convolution fusion | flops 8589934592 | bytes 42991616 | tf_op jit(solution)/shard_map/rihc,rtc->rhit/dot_general | solution.py:107
  150.5 21.9 %fusion.96 = (f32[128,64]{0,1:T(8,128)S(1)}, f32[1,128,64,1024]{3,1,2,0:T(8,128)}) fusion(f32[64,128,1024]{2,1,0:T(8,128)} %fusion.12, bf16[1,1024,64]{1,2,0:T(8,128)(2,1)S(1)} %copy-done.4, bf16[1,64,128,64]{2,3,1,0:T(8,128)(2,1)S(1)} %copy-done.3, pred[1024]{0:T(1024)(128)(4,1)S(1)} %add_compare_fusion), kind=kOutput, calls=%fused_computation.168 | convolution fusion | flops 1107288064 | bytes 68322304 | tf_op jit(solution)/shard_map/rihe,rte->rhit/dot_general | solution.py:110
  172.5 15.1 %all_to_all.5 = f32[16,1,128,64]{2,3,1,0:T(8,128)S(1)} all-to-all(f32[16,1,128,64]{2,3,1,0:T(8,128)S(1)} %broadcast_in_dim.37), channel_id=1, replica_groups=mesh['seq_0'=4,'seq_1'=4,'batch_0'=4,'batch_1'=2] {'seq_0','seq_1'}, dimensions={0} | all-to-all | bytes 1048576 | tf_op jit(solution)/shard_map/all_to_all | solution.py:27
  187.7 18.7 %fusion.7 = f32[1,128,64,512]{3,1,2,0:T(8,128)} fusion(f32[1,128,64,1024]{3,1,2,0:T(8,128)} %get-tuple-element.19, f32[128,64]{0,1:T(8,128)S(1)} %reduce_max.38, bf16[1,1024,512]{2,1,0:T(8,128)(2,1)S(1)} %copy-done), kind=kOutput, calls=%fused_computation.10 | convolution fusion | flops 8606711808 | bytes 51412992 | tf_op jit(solution)/shard_map/rhit,rtc->rhic/dot_general | solution.py:129
  206.5 0.6 copy-done.12
  207.0 0.6 dynamic-slice.5
  208.4 1.0 fusion.24
  209.5 14.9 %fusion.1 = f32[128,64]{0,1:T(8,128)S(1)} fusion(f32[1,128,64,1024]{3,1,2,0:T(8,128)} %get-tuple-element.19, f32[128,64]{0,1:T(8,128)S(1)} %reduce_max.38), kind=kLoop, calls=%fused_computation.5 | loop fusion | flops 16769024 | bytes 33619968 | tf_op jit(solution)/shard_map/reduce_sum | solution.py:128
  224.6 58.5 %all-reduce = f32[1,128,64]{2,1,0:T(8,128)S(1)} all-reduce(f32[1,128,64]{2,1,0:T(8,128)S(1)} %copy.53), channel_id=7, replica_groups=mesh['seq_0'=4,'seq_1'=4,'batch_0'=4,'batch_1'=2] {'seq_0','seq_1'}, use_global_device_ids=true, to_apply=%region_5.6.clone | all-reduce | flops 8192 | bytes 65536
  283.4 33.9 %reduce-scatter.3.cloned.1.call-done = f32[1,8,64,512]{3,1,2,0:T(8,128)} async-done(((f32[1,128,64,512]{3,1,2,0:T(8,128)}), f32[1,8,64,512]{3,1,2,0:T(8,128)}) %reduce-scatter.3.cloned.1.call-update) | async-done | bytes 1048592 | tf_op jit(solution)/shard_map/reduce_scatter | solution.py:146
  317.3 1.5 fusion.15
  318.9 0.4 fusion.19
  319.4 7.9 %fusion.27 = f32[64,7168]{1,0:T(8,128)S(1)} fusion(bf16[1024,7168]{1,0:T(8,128)(2,1)} %param.25, bf16[8,8,8,128]{3,2,1,0:T(8,128)(2,1)S(1)} %bitcast.377), kind=kOutput, calls=%fused_computation.45 | convolution fusion | flops 939524096 | bytes 16646144 | tf_op jit(solution)/shard_map/dot_general | solution.py:157
  327.4 1.1 add.354
  328.5 1.2 copy-done.2
  329.8 54.3 %all-reduce.4.cloned.1.call-done = f32[64,7168]{1,0:T(8,128)} async-done(((f32[64,7168]{1,0:T(8,128)}), f32[64,7168]{1,0:T(8,128)}) %all-reduce.4.cloned.1.call-update) | async-done | bytes 1835024 | tf_op jit(solution)/shard_map/psum | solution.py:163
  384.2 56.7 %all-reduce.6.cloned.1.call-done = f32[64,7168]{1,0:T(8,128)} async-done(((f32[64,7168]{1,0:T(8,128)}), f32[64,7168]{1,0:T(8,128)}) %all-reduce.6.cloned.1.call-update) | async-done | bytes 1835024 | tf_op jit(solution)/shard_map/psum | solution.py:163
  440.9 1.7 multiply_reduce_fusion
  442.6 2.7 multiply_convert_fusion
  446.2 1.6 dynamic-slice_convert_fusion
  447.9 43.0 %all-gather.13.cloned.1.call-done = bf16[512,7168]{1,0:T(8,128)(2,1)} async-done(((bf16[64,7168]{1,0:T(8,128)(2,1)}), bf16[512,7168]{1,0:T(8,128)(2,1)}) %all-gather.13.cloned.1.call-update) | async-done | bytes 7340048 | tf_op jit(solution)/shard_map/all_gather | solution.py:175
  490.8 8.5 %fusion.98 = (f32[512]{0:T(512)S(1)}, f32[512,512]{0,1:T(8,128)S(1)}) fusion(bf16[512,7168]{1,0:T(8,128)(2,1)} %all-gather.13.cloned.1.call-done, bf16[512,7168]{1,0:T(8,128)(2,1)} %param.27), kind=kOutput, calls=%fused_computation.170 | convolution fusion | flops 3758358016 | bytes 15730688 | tf_op jit(solution)/shard_map/rd,vd->rv/dot_general | solution.py:173
  499.4 0.3 copy.58
  499.7 0.2 exponential_reduce_fusion
  499.9 1.6 gather_fusion
  501.5 0.3 select_reduce_fusion
  501.8 9.6 %all-gather.4 = f32[4,3,512]{2,1,0:T(4,128)S(1)} all-gather(f32[1,3,512]{2,1,0:T(4,128)S(1)} %maximum_bitcast_fusion.1), channel_id=2, replica_groups=mesh['seq_0'=4,'seq_1'=4,'batch_0'=4,'batch_1'=2] {'seq_0'}, dimensions={0}, use_global_device_ids=true | all-gather | bytes 30720 | tf_op jit(solution)/shard_map/all_gather | solution.py:43
  511.4 9.5 %all-gather.5 = f32[4,3,512]{2,1,0:T(4,128)S(1)} all-gather(f32[1,3,512]{2,1,0:T(4,128)S(1)} %maximum_bitcast_fusion.2), channel_id=3, replica_groups=mesh['seq_0'=4,'seq_1'=4,'batch_0'=4,'batch_1'=2] {'seq_1'}, dimensions={0}, use_global_device_ids=true | all-gather | bytes 30720 | tf_op jit(solution)/shard_map/all_gather | solution.py:43
  521.0 9.0 %all-gather.6 = f32[4,3,512]{2,1,0:T(4,128)S(1)} all-gather(f32[1,3,512]{2,1,0:T(4,128)S(1)} %maximum_bitcast_fusion.3), channel_id=4, replica_groups=mesh['seq_0'=4,'seq_1'=4,'batch_0'=4,'batch_1'=2] {'batch_0'}, dimensions={0}, use_global_device_ids=true | all-gather | bytes 30720 | tf_op jit(solution)/shard_map/all_gather | solution.py:43
  530.1 10.2 %all-gather.7 = f32[2,3,512]{2,1,0:T(4,128)S(1)} all-gather(f32[1,3,512]{2,1,0:T(4,128)S(1)} %maximum_bitcast_fusion.4), channel_id=5, replica_groups=mesh['seq_0'=4,'seq_1'=4,'batch_0'=4,'batch_1'=2] {'batch_1'}, dimensions={0}, use_global_device_ids=true | all-gather | bytes 18432 | tf_op jit(solution)/shard_map/all_gather | solution.py:43
  540.3 3.5 gather_fusion.1
  544.0 1.1 fusion.89
  (80 shorter events, 2.8 us)
Async XLA Ops:
  7.2 113.3 %copy-start = (bf16[1,1024,512]{2,1,0:T(8,128)(2,1)S(1)}, bf16[1,1024,512]{2,1,0:T(8,128)(2,1)}, u32[]{:S(2)}) copy-start(bf16[1,1024,512]{2,1,0:T(8,128)(2,1)} %param.20) | copy-start | bytes 3145732
  7.2 92.3 %copy-start.5 = (bf16[1,64,512]{2,1,0:T(8,128)(2,1)S(1)}, bf16[1,64,512]{2,1,0:T(8,128)(2,1)}, u32[]{:S(2)}) copy-start(bf16[1,64,512]{2,1,0:T(8,128)(2,1)} %param.22) | copy-start | bytes 196612
  7.2 87.5 %all-gather.11.cloned.1.call-start = ((), (), s32[]{:S(2)}) async-start(), calls=%async_computation.2 | async-start | bytes 11141120 | tf_op jit(solution)/shard_map/all_gather | solution.py:22
  10.8 306.5 %reduce-scatter.3.cloned.1.call-start = ((), (), s32[]{:S(2)}) async-start(), calls=%async_computation.3 | async-start | bytes 17825792 | tf_op jit(solution)/shard_map/reduce_scatter | solution.py:146
  96.5 10.4 %copy-start.8 = (bf16[1,64,64]{2,1,0:T(8,128)(2,1)S(1)}, bf16[1,64,64]{2,1,0:T(8,128)(2,1)}, u32[]{:S(2)}) copy-start(bf16[1,64,64]{2,1,0:T(8,128)(2,1)} %param.23) | copy-start | bytes 24580
  120.5 30.0 %copy-start.3 = (bf16[1,64,128,64]{2,3,1,0:T(8,128)(2,1)S(1)}, bf16[1,64,128,64]{2,3,1,0:T(8,128)(2,1)}, u32[]{:S(2)}) copy-start(bf16[1,64,128,64]{2,3,1,0:T(8,128)(2,1)} %copy.69) | copy-start | bytes 3145732
  120.5 30.0 %copy-start.4 = (bf16[1,1024,64]{1,2,0:T(8,128)(2,1)S(1)}, bf16[1,1024,64]{1,2,0:T(8,128)(2,1)}, u32[]{:S(2)}) copy-start(bf16[1,1024,64]{1,2,0:T(8,128)(2,1)} %param.21) | copy-start | bytes 393220
  206.4 0.7 copy-start.12
  206.4 177.7 %all-reduce.4.cloned.1.call-start = ((), (), s32[]{:S(2)}) async-start(), calls=%async_computation.4 | async-start | bytes 3670016 | tf_op jit(solution)/shard_map/psum | solution.py:163
  209.5 109.3 %copy-start.11 = (bf16[8,512,128]{2,1,0:T(8,128)(2,1)S(1)}, bf16[8,512,128]{2,1,0:T(8,128)(2,1)}, u32[]{:S(2)}) copy-start(bf16[8,512,128]{2,1,0:T(8,128)(2,1)} %param.19) | copy-start | bytes 3145732
  319.3 7.9 %copy-start.6 = (bf16[64,448]{1,0:T(8,128)(2,1)S(1)}, bf16[64,448]{1,0:T(8,128)(2,1)}, u32[]{:S(2)}) copy-start(bf16[64,448]{1,0:T(8,128)(2,1)} %param.24) | copy-start | bytes 172036
  319.3 123.3 %copy-start.7 = (f32[7168]{0:T(1024)S(1)}, f32[7168]{0:T(1024)}, u32[]{:S(2)}) copy-start(f32[7168]{0:T(1024)} %param.26) | copy-start | bytes 86020
  327.2 118.7 %copy-start.9 = (s32[8,64]{1,0:T(8,128)S(1)}, s32[8,64]{1,0:T(8,128)}, u32[]{:S(2)}) copy-start(s32[8,64]{1,0:T(8,128)} %param.29) | copy-start | bytes 6148
  327.2 118.8 %copy-start.10 = (s32[8,64]{1,0:T(8,128)S(1)}, s32[8,64]{1,0:T(8,128)}, u32[]{:S(2)}) copy-start(s32[8,64]{1,0:T(8,128)} %param.28) | copy-start | bytes 6148
  328.5 1.2 copy-start.2
  329.7 111.1 %all-reduce.6.cloned.1.call-start = ((), (), s32[]{:S(2)}) async-start(), calls=%async_computation.5 | async-start | bytes 3670016 | tf_op jit(solution)/shard_map/psum | solution.py:163
  384.1 106.7 %all-gather.13.cloned.1.call-start = ((), (), s32[]{:S(2)}) async-start(), calls=%async_computation.6 | async-start | bytes 8257536 | tf_op jit(solution)/shard_map/all_gather | solution.py:175
  490.8 54.3 %copy-start.1 = (bf16[1,1024,512]{2,1,0:T(8,128)(2,1)S(1)}, bf16[1,1024,512]{2,1,0:T(8,128)(2,1)}, u32[]{:S(2)}) copy-start(bf16[1,1024,512]{2,1,0:T(8,128)(2,1)} %param.20) | copy-start | bytes 3145732
Sparse Core Ops, SparseCore 0:
  10.9 83.7 all-gather.10
  206.5 110.7 reduce-scatter.2
  329.8 54.2 all-reduce.3
  386.3 54.4 all-reduce.5
  445.4 45.3 all-gather.12
